TPU v7x, 512 devices: a whole 4x4x16 slice. The times are simulated.
512 devices in a mesh: grp: 16 (over y, x), tok: 32 (over z, core).
Axes of the slice: x: 4, y: 4, z: 16, core: 2. Of those that a mesh axis runs over, the one named last changes fastest.
Arguments:
- hidden_in: bfloat16 [16, 4096, 1024], P('grp', 'tok'), may hold values from -6 to 6
- lengths: int32 [16, 3], P('grp'), may hold values from 1 to 3072, 4096 in all within a row
- prefix_cache: bfloat16 [16, 512, 512], P('grp', 'tok'), may hold values from -2600 to 2600
- routes: int32 [16, 4096, 8], P('grp', 'tok'), may hold values from 0 to 31, all different within a row; in each aligned block of 128 rows (0 to 127, 128 to 255, ..., all dimensions but the last counted through in order) at most 40 rows name the same one
- gates: float32 [16, 4096, 8], P('grp', 'tok'), may hold values from 0.05 to 0.4
- attn_gain: float32 [1024], replicated, may hold values from 0.1 to 1.9
- w_qkv: bfloat16 [1024, 1024], P('grp', 'tok'), may hold values from -0.75 to 0.75
- w_out: bfloat16 [512, 1024], P('grp', 'tok'), may hold values from -0.25 to 0.25
- moe_gain: float32 [1024], replicated, may hold values from 0.1 to 1.9
- expert_gate_up: bfloat16 [32, 1024, 1024], P('tok', 'grp'), may hold values from -0.1875 to 0.1875
- expert_down: bfloat16 [32, 512, 1024], P('tok', 'grp'), may hold values from -0.25 to 0.25
Outputs:
- hidden_out: bfloat16 [16, 4096, 1024], P('grp', 'tok')
- suffix_cache: bfloat16 [16, 4096, 512], P('grp', 'tok')
Inputs may be any that keep to these rules, and one draw needn't show every extreme that they name: Each group's 3 lengths sum to 4096; no request is longer than 3072 tokens, and some request of every draw has exactly 3072. `routes`: each token names 8 different experts. Among the 128 tokens of one device no expert is named more than 40 times, a bound that some block reaches.
All inputs are finite; a program needn't handle non-finite values.
Results may differ from a plain program's by a relative error of at most 0.02.
Values may be sent and summed in bfloat16 or wider, within the bound.
A program may use at most 128 MiB of HBM per device.

v0:
```python
import jax
import jax.numpy as jnp
from jax import lax
from jax.sharding import PartitionSpec as P

HEADS = 8
KV_HEADS = 4
HEAD_DIM = 64
FF = 512
EXPERTS = 32
TOP = 8
CAP = 40
epsilon = 1e-05
score_scale = 0.015625
rope_base = 10000.0
big_negative = -1e30


def rms_scale(values, gain):
    values = values.astype(jnp.float32)
    mean_square = jnp.mean(values * values, axis=-1, keepdims=True)
    return values * lax.rsqrt(mean_square + epsilon) * gain


def request_layout(group_lengths, token_index):
    ends = jnp.cumsum(group_lengths)
    starts = ends - group_lengths
    segment = jnp.sum((token_index[:, None] >= ends[None, :]).astype(jnp.int32), axis=1)
    match = segment[:, None] == jnp.arange(group_lengths.shape[0], dtype=jnp.int32)[None, :]
    offset = token_index - jnp.sum(jnp.where(match, starts[None, :], 0), axis=1)
    return (segment, offset)


def rotate(values, position):
    half_width = values.shape[-1] // 2
    frequency = rope_base ** (-jnp.arange(half_width, dtype=jnp.float32) * 2.0 / values.shape[-1])
    angle = position.astype(jnp.float32)[:, None] * frequency[None, :]
    cosine = jnp.cos(angle)[:, None, :]
    sine = jnp.sin(angle)[:, None, :]
    first = values[..., :half_width]
    second = values[..., half_width:]
    return jnp.concatenate(
        [first * cosine - second * sine, second * cosine + first * sine], axis=-1
    )


def attend(carry, grouped, keys_values, allowed):
    best, total, mixed = carry
    key_count = keys_values.shape[0]
    key_width = KV_HEADS * HEAD_DIM
    key_heads = keys_values[:, :key_width].reshape(key_count, KV_HEADS, HEAD_DIM).transpose(1, 0, 2)
    value_heads = (
        keys_values[:, key_width:].reshape(key_count, KV_HEADS, HEAD_DIM).transpose(1, 0, 2)
    )
    scores = (
        jnp.einsum("kqd,knd->kqn", grouped, key_heads, preferred_element_type=jnp.float32)
        * score_scale
    )
    if allowed is not None:
        row_count = grouped.shape[1]
        share = row_count // allowed.shape[0]
        mask = jnp.broadcast_to(allowed[:, None, :], (allowed.shape[0], share, key_count)).reshape(
            row_count, key_count
        )
        scores = jnp.where(mask[None], scores, big_negative)
    new_best = jnp.maximum(best, jnp.max(scores, axis=-1))
    factor = jnp.exp(best - new_best)
    probs = jnp.exp(scores - new_best[..., None])
    total = total * factor + jnp.sum(probs, axis=-1)
    mixed = mixed * factor[..., None] + jnp.einsum(
        "kqn,knd->kqd", probs.astype(jnp.bfloat16), value_heads, preferred_element_type=jnp.float32
    )
    return (new_best, total, mixed)


def local(
    hidden_in,
    lengths,
    prefix_cache,
    routes,
    gates,
    attn_gain,
    w_qkv,
    w_out,
    moe_gain,
    expert_gate_up,
    expert_down,
):
    tokens_here = hidden_in[0]
    tok_count = tokens_here.shape[0]
    axis_count = lax.axis_size("tok")
    device_place = lax.axis_index("tok")
    group_lengths = lengths[0]
    token_index = device_place * tok_count + jnp.arange(tok_count, dtype=jnp.int32)
    segment, offset = request_layout(group_lengths, token_index)
    position = prefix_cache.shape[1] * axis_count + offset
    query_width = HEADS * HEAD_DIM
    key_width = KV_HEADS * HEAD_DIM
    group_share = HEADS // KV_HEADS
    normed = rms_scale(tokens_here, attn_gain).astype(jnp.bfloat16)
    columns = lax.all_gather(w_qkv, "tok", axis=1, tiled=True)
    sliced = normed
    projected = jnp.dot(
        sliced,
        lax.all_gather(columns, "grp", axis=0, tiled=True),
        preferred_element_type=jnp.float32,
    )
    query = rotate(projected[:, :query_width].reshape(tok_count, HEADS, HEAD_DIM), position).astype(
        jnp.bfloat16
    )
    keys_new = rotate(
        projected[:, query_width : query_width + key_width].reshape(tok_count, KV_HEADS, HEAD_DIM),
        position,
    ).astype(jnp.bfloat16)
    values_new = projected[:, query_width + key_width :].astype(jnp.bfloat16)
    suffix_cache = jnp.concatenate([keys_new.reshape(tok_count, key_width), values_new], axis=1)
    row_count = tok_count * group_share
    grouped = (
        query.reshape(tok_count, KV_HEADS, group_share, HEAD_DIM)
        .transpose(1, 0, 2, 3)
        .reshape(KV_HEADS, row_count, HEAD_DIM)
    )
    start_carry = (
        jnp.full((KV_HEADS, row_count), big_negative, jnp.float32),
        jnp.zeros((KV_HEADS, row_count), jnp.float32),
        jnp.zeros((KV_HEADS, row_count, HEAD_DIM), jnp.float32),
    )
    carry = attend(
        start_carry, grouped, lax.all_gather(prefix_cache[0], "tok", axis=0, tiled=True), None
    )
    piece = lax.all_gather(suffix_cache, "tok", axis=0, tiled=True)
    key_index = jnp.arange(piece.shape[0], dtype=jnp.int32)
    key_segment, key_offset = request_layout(group_lengths, key_index)
    earlier = key_index[None, :] <= token_index[:, None]
    same_request = key_segment[None, :] == segment[:, None]
    carry = attend(carry, grouped, piece, earlier & same_request & (key_index[None, :] >= 0))
    best, total, mixed = carry
    attended = (mixed / total[..., None]).reshape(KV_HEADS, tok_count, group_share, HEAD_DIM)
    attended = attended.transpose(1, 0, 2, 3).reshape(tok_count, query_width).astype(jnp.bfloat16)
    out_columns = lax.all_gather(w_out, "tok", axis=1, tiled=True)
    sliced = attended
    projected_out = jnp.dot(
        sliced,
        lax.all_gather(out_columns, "grp", axis=0, tiled=True),
        preferred_element_type=jnp.float32,
    )
    after_attention = tokens_here.astype(jnp.float32) + projected_out
    moe_in = rms_scale(after_attention, moe_gain).astype(jnp.bfloat16)
    model_width = moe_in.shape[1]
    flat_routes = routes[0].reshape(-1)
    onehot = (flat_routes[:, None] == jnp.arange(EXPERTS, dtype=jnp.int32)[None, :]).astype(
        jnp.int32
    )
    slot_rank = jnp.sum(jnp.cumsum(onehot, axis=0) * onehot, axis=1) - 1
    slot_index = flat_routes * CAP + slot_rank
    source_token = jnp.arange(flat_routes.shape[0], dtype=jnp.int32) // TOP
    outgoing = (
        jnp.zeros((EXPERTS * CAP, model_width), jnp.bfloat16)
        .at[slot_index]
        .set(moe_in[source_token])
    )
    arrived = lax.all_to_all(
        outgoing.reshape(EXPERTS, CAP, model_width), "tok", split_axis=0, concat_axis=1, tiled=True
    )
    sliced = arrived
    hidden_pair = jnp.einsum(
        "erd,edf->erf",
        sliced,
        lax.all_gather(expert_gate_up, "grp", axis=1, tiled=True),
        preferred_element_type=jnp.float32,
    )
    activated = (jax.nn.silu(hidden_pair[..., :FF]) * hidden_pair[..., FF:]).astype(jnp.bfloat16)
    sliced = activated
    expert_result = jnp.einsum(
        "erf,efd->erd",
        sliced,
        lax.all_gather(expert_down, "grp", axis=1, tiled=True),
        preferred_element_type=jnp.float32,
    ).astype(jnp.bfloat16)
    returned = lax.all_to_all(
        expert_result, "tok", split_axis=1, concat_axis=0, tiled=True
    ).reshape(EXPERTS * CAP, -1)
    weighted = returned[slot_index].astype(jnp.float32) * gates[0].reshape(-1)[:, None]
    moe_out = jnp.sum(weighted.reshape(tok_count, TOP, -1), axis=1)
    hidden_out = (after_attention + moe_out).astype(jnp.bfloat16)
    return (hidden_out[None], suffix_cache[None])


def solution(mesh):
    return jax.shard_map(
        local,
        mesh=mesh,
        in_specs=(
            P("grp", "tok", None),
            P("grp", None),
            P("grp", "tok", None),
            P("grp", "tok", None),
            P("grp", "tok", None),
            P(),
            P("grp", "tok"),
            P("grp", "tok"),
            P(),
            P("tok", "grp", None),
            P("tok", "grp", None),
        ),
        out_specs=(P("grp", "tok", None), P("grp", "tok", None)),
        check_vma=False,
    )
```

profile of v0, /device:TPU:32, one launch (start us, length us, event | category | flops | bytes accessed | tf_op | source)
XLA Modules:
  0.0 593.4 jit_solution(6562197188762396571)
XLA Ops:
  7.2 35.0 %all_gather.24 = bf16[64,1024]{0,1:T(8,128)(2,1)S(1)} all-gather(bf16[64,32]{0,1:T(8,128)(2,1)} %param.17), channel_id=1, replica_groups=mesh['grp'=16,'tok'=32] {'tok'}, dimensions={1}, use_global_device_ids=true | all-gather | bytes 135168 | tf_op jit(solution)/shard_map/all_gather | solution.py:101
  46.1 55.2 %all-gather.7.cloned.1.call-done = bf16[1024,1024]{1,0:T(8,128)(2,1)} async-done(((bf16[64,1024]{1,0:T(8,128)(2,1)}), bf16[1024,1024]{1,0:T(8,128)(2,1)}) %all-gather.7.cloned.1.call-update) | async-done | bytes 2097168 | tf_op jit(solution)/shard_map/all_gather | solution.py:105
  101.3 2.2 fusion.30
  105.4 30.6 %all_gather.28 = bf16[32,1024]{0,1:T(8,128)(2,1)S(1)} all-gather(bf16[32,32]{0,1:T(8,128)(2,1)S(1)} %copy.120), channel_id=1, replica_groups=mesh['grp'=16,'tok'=32] {'tok'}, dimensions={1}, use_global_device_ids=true | all-gather | bytes 67584 | tf_op jit(solution)/shard_map/all_gather | solution.py:140
  137.7 2.4 broadcast_in_dim.41
  140.2 2.6 broadcast_in_dim.42
  142.7 31.0 %all-gather = bf16[1,512,512]{2,1,0:T(8,128)(2,1)S(1)} all-gather(bf16[1,16,512]{2,1,0:T(8,128)(2,1)S(1)} %copy-done.5), channel_id=2, replica_groups=mesh['grp'=16,'tok'=32] {'tok'}, dimensions={1}, use_global_device_ids=true | all-gather | bytes 540672 | tf_op jit(solution)/shard_map/all_gather | solution.py:129
  175.0 9.2 %reduce-window.11 = s32[32,8,128]{2,1,0:T(8,128)S(1)} reduce-window(s32[32,8,128]{2,1,0:T(8,128)S(1)} %fusion.37, s32[]{:T(128)} %constant.34.clone.1), window={size=1x1x128 pad=0_0x0_0x127_0}, to_apply=%region_9.10 | reduce-window | flops 4161536 | bytes 262148 | tf_op jit(solution)/shard_map/reduce-window.1
  186.0 1.8 multiply_reduce_fusion
  187.8 3.8 fusion.45
  191.6 2.9 copy.117
  194.6 2.9 copy.115
  197.5 3.5 fusion
  201.0 4.4 fusion.1
  205.4 1.9 copy-done
  207.9 11.2 %fusion.3 = f32[4,256,64]{1,2,0:T(8,128)} fusion(bf16[4,4096,64]{1,2,0:T(8,128)(2,1)} %bitcast.105, f32[4,256,4096]{2,1,0:T(8,128)} %copy-done, f32[4,256]{1,0:T(4,128)S(1)} %get-tuple-element.15, pred[256,4096]{1,0:T(8,128)(4,1)S(1)} %broadcast_in_dim.42), kind=kOutput, calls=%fused_computation.8 | convolution fusion | flops 553648128 | bytes 20189184 | tf_op jit(solution)/shard_map/kqn,knd->kqd/dot_general | solution.py:70
  221.0 16.5 %all-gather.11.cloned.1.call-done = bf16[512,1024]{1,0:T(8,128)(2,1)} async-done(((bf16[32,1024]{1,0:T(8,128)(2,1)}), bf16[512,1024]{1,0:T(8,128)(2,1)}) %all-gather.11.cloned.1.call-update) | async-done | bytes 1048592 | tf_op jit(solution)/shard_map/all_gather | solution.py:144
  239.3 14.7 %scatter_custom_fusion = bf16[1280,1024]{1,0:T(8,128)(2,1)} fusion(s32[1024]{0:T(1024)S(1)} %bitcast.118, bf16[128,1024]{1,0:T(8,128)(2,1)S(1)} %multiply_convert_fusion, s32[1024]{0:T(1024)S(1)} %broadcast_clamp_fusion.1, bf16[]{:T(256)} %constant.67.clone.1), kind=kCustom, calls=%fused_computation.19 | custom fusion | bytes 2621442 | tf_op jit(solution)/shard_map/scatter | solution.py:160
  254.1 12.8 %all-to-all-start = ((bf16[32,40,1024]{2,1,0:T(8,128)(2,1)}), bf16[32,40,1024]{2,1,0:T(8,128)(2,1)S(1)}, u32[]{:S(2)}, u32[]{:S(2)}) async-start(bf16[32,40,1024]{2,1,0:T(8,128)(2,1)} %bitcast.31), calls=%async_computation | async-start | bytes 5242880 | tf_op jit(solution)/shard_map/all_to_all | solution.py:162
  268.0 61.4 %all-gather.13.cloned.1.call-done = bf16[1,1024,1024]{2,1,0:T(8,128)(2,1)} async-done(((bf16[1,64,1024]{2,1,0:T(8,128)(2,1)}), bf16[1,1024,1024]{2,1,0:T(8,128)(2,1)}) %all-gather.13.cloned.1.call-update) | async-done | bytes 2097168 | tf_op jit(solution)/shard_map/all_gather | solution.py:169
  329.4 60.2 %all-to-all-done = bf16[32,40,1024]{2,1,0:T(8,128)(2,1)S(1)} async-done(((bf16[32,40,1024]{2,1,0:T(8,128)(2,1)}), bf16[32,40,1024]{2,1,0:T(8,128)(2,1)S(1)}, u32[]{:S(2)}, u32[]{:S(2)}) %all-to-all-start) | async-done | bytes 2621472 | tf_op jit(solution)/shard_map/all_to_all | solution.py:162
  389.6 6.2 %convolution_bitcast_fusion = f32[1,1280,1024]{2,1,0:T(8,128)} fusion(bf16[1280,1024]{1,0:T(8,128)(2,1)S(1)} %bitcast.104, bf16[1,1024,1024]{2,1,0:T(8,128)(2,1)} %all-gather.13.cloned.1.call-done), kind=kOutput, calls=%fused_computation.10 | convolution fusion | flops 2684354560 | bytes 9961472 | tf_op jit(solution)/shard_map/erd,edf->erf/dot_general | solution.py:166
  395.8 4.4 fusion.7
  400.2 18.2 %copy.137 = bf16[1,1280,1024]{2,0,1:T(2,128)(2,1)} copy(bf16[1,1280,1024]{2,1,0:T(8,128)(2,1)S(1)} %fusion.7) | data formatting | bytes 5242880 | tf_op jit(solution)/shard_map/convert_element_type | solution.py:179
  418.9 15.6 %reduce = bf16[1280,1024]{1,0:T(8,128)(2,1)S(1)} reduce(bf16[1280,1,1024]{2,1,0:T(2,128)(2,1)} %bitcast.99, bf16[]{:T(256)} %broadcast.297), dimensions={1}, to_apply=%bitcast.97.reduce_sub_computation | reduce | bytes 5242882
  434.4 3.0 reshape.386
  437.4 6.9 %all-to-all-start.1 = ((bf16[32,2,20480]{2,1,0:T(2,128)(2,1)}), bf16[32,2,20480]{2,1,0:T(2,128)(2,1)S(1)}, u32[]{:S(2)}, u32[]{:S(2)}) async-start(bf16[32,2,20480]{2,1,0:T(2,128)(2,1)} %reshape.386), calls=%async_computation.1 | async-start | bytes 5242880 | tf_op jit(solution)/shard_map/all_to_all | solution.py:180
  444.5 122.6 %all-to-all-done.1 = bf16[32,2,20480]{2,1,0:T(2,128)(2,1)S(1)} async-done(((bf16[32,2,20480]{2,1,0:T(2,128)(2,1)}), bf16[32,2,20480]{2,1,0:T(2,128)(2,1)S(1)}, u32[]{:S(2)}, u32[]{:S(2)}) %all-to-all-start.1) | async-done | bytes 2621472 | tf_op jit(solution)/shard_map/all_to_all | solution.py:180
  567.1 7.2 %reshape.387 = bf16[1280,1,1024]{2,1,0:T(2,128)(2,1)} reshape(bf16[32,2,20480]{2,1,0:T(2,128)(2,1)S(1)} %all-to-all-done.1) | data formatting | bytes 5242880
  574.3 3.5 copy.136
  577.8 5.4 gather_fusion
  583.2 2.9 fusion.6
  (94 shorter events, 17.1 us)
Async XLA Ops:
  7.2 94.1 %all-gather.7.cloned.1.call-start = ((), (), s32[]{:S(2)}) async-start(), calls=%async_computation.2 | async-start | bytes 2228224 | tf_op jit(solution)/shard_map/all_gather | solution.py:105
  42.3 63.1 %copy-start.7 = (bf16[32,32]{1,0:T(8,128)(2,1)S(1)}, bf16[32,32]{1,0:T(8,128)(2,1)}, u32[]{:S(2)}) copy-start(bf16[32,32]{1,0:T(8,128)(2,1)} %param.18) | copy-start | bytes 6148
  43.1 144.7 %all-gather.9.cloned.1.call-start = ((), (), s32[]{:S(2)}) async-start(), calls=%async_computation.3 | async-start | bytes 4325376 | tf_op jit(solution)/shard_map/all_gather | solution.py:131
  46.1 90.9 %copy-start.6 = (s32[1,128,8]{1,2,0:T(8,128)S(1)}, s32[1,128,8]{1,2,0:T(8,128)}, u32[]{:S(2)}) copy-start(s32[1,128,8]{1,2,0:T(8,128)} %param.14) | copy-start | bytes 12292
  103.5 0.8 copy-start.3
  105.3 132.3 %all-gather.11.cloned.1.call-start = ((), (), s32[]{:S(2)}) async-start(), calls=%async_computation.4 | async-start | bytes 1114112 | tf_op jit(solution)/shard_map/all_gather | solution.py:144
  137.7 5.0 copy-start.5
  142.7 42.0 %slice-start = ((f32[128,1024]{1,0:T(8,128)}), f32[128,512]{1,0:T(8,128)S(1)}, s32[]{:S(2)}) async-start(f32[128,1024]{1,0:T(8,128)} %copy-done.3), calls=%async_computation.7 | async-start | bytes 524288 | tf_op jit(solution)/shard_map/slice | solution.py:108
  201.0 6.3 %copy-start = (f32[4,256,4096]{2,1,0:T(8,128)}, f32[4,256,4096]{2,1,0:T(8,128)S(1)}, u32[]{:S(2)}) copy-start(f32[4,256,4096]{2,1,0:T(8,128)S(1)} %get-tuple-element.22) | copy-start | bytes 50331652
  201.0 6.3 %copy-start.1 = (f32[4,256,512]{2,1,0:T(8,128)S(1)}, f32[4,256,512]{2,1,0:T(8,128)}, u32[]{:S(2)}) copy-start(f32[4,256,512]{2,1,0:T(8,128)} %get-tuple-element.20) | copy-start | bytes 6291460
  207.9 11.2 %copy-start.4 = (bf16[512,256]{0,1:T(8,128)(2,1)S(1)}, bf16[512,256]{0,1:T(8,128)(2,1)}, u32[]{:S(2)}) copy-start(bf16[512,256]{0,1:T(8,128)(2,1)} %copy.112) | copy-start | bytes 786436
  219.1 18.4 %copy-start.2 = (bf16[1,128,1024]{2,1,0:T(8,128)(2,1)S(1)}, bf16[1,128,1024]{2,1,0:T(8,128)(2,1)}, u32[]{:S(2)}) copy-start(bf16[1,128,1024]{2,1,0:T(8,128)(2,1)} %param.11) | copy-start | bytes 786436
  219.1 20.1 %copy-start.8 = (f32[1024]{0:T(1024)S(1)}, f32[1024]{0:T(1024)}, u32[]{:S(2)}) copy-start(f32[1024]{0:T(1024)} %param.19) | copy-start | bytes 12292
  254.1 135.6 %all-to-all-start = ((bf16[32,40,1024]{2,1,0:T(8,128)(2,1)}), bf16[32,40,1024]{2,1,0:T(8,128)(2,1)S(1)}, u32[]{:S(2)}, u32[]{:S(2)}) async-start(bf16[32,40,1024]{2,1,0:T(8,128)(2,1)} %bitcast.31), calls=%async_computation | async-start | bytes 5242880 | tf_op jit(solution)/shard_map/all_to_all | solution.py:162
  266.9 62.5 %all-gather.13.cloned.1.call-start = ((), (), s32[]{:S(2)}) async-start(), calls=%async_computation.5 | async-start | bytes 2228224 | tf_op jit(solution)/shard_map/all_gather | solution.py:169
  267.5 128.3 %all-gather.15.cloned.1.call-start = ((), (), s32[]{:S(2)}) async-start(), calls=%async_computation.6 | async-start | bytes 1114112 | tf_op jit(solution)/shard_map/all_gather | solution.py:177
  437.4 6.9 %copy-start.9 = (f32[1,128,8]{1,2,0:T(8,128)S(1)}, f32[1,128,8]{1,2,0:T(8,128)}, u32[]{:S(2)}) copy-start(f32[1,128,8]{1,2,0:T(8,128)} %param.15) | copy-start | bytes 12292
  437.4 129.7 %all-to-all-start.1 = ((bf16[32,2,20480]{2,1,0:T(2,128)(2,1)}), bf16[32,2,20480]{2,1,0:T(2,128)(2,1)S(1)}, u32[]{:S(2)}, u32[]{:S(2)}) async-start(bf16[32,2,20480]{2,1,0:T(2,128)(2,1)} %reshape.386), calls=%async_computation.1 | async-start | bytes 5242880 | tf_op jit(solution)/shard_map/all_to_all | solution.py:180
Sparse Core Ops, SparseCore 0:
  43.2 58.0 all-gather.6
  105.4 73.6 all-gather.8
  182.1 55.3 all-gather.10
  270.4 58.9 all-gather.12
  332.3 57.4 all-gather.14
where the time goes:
time: 594 us; the launch traced here: 593 us
  waiting for transfers between devices  317 us (53%)
  blocking collectives  96.7 us (16%)
  local copies, waits for them, and re-layouts  74.3 us (13%)
  other arithmetic  38.8 us (7%)
  matrix products  32.4 us (5%)
  starting transfers between devices  19.9 us (3%)
  between operations  14.2 us (2%)
    all_to_all x1, waiting for transfers between devices, local(): lax.all_to_all(expert_result, 'tok', split_axis=1, concat_axis=0, tiled=T...  123 us
    all_gather x1, waiting for transfers between devices, local(): lax.all_gather(expert_gate_up, 'grp', axis=1, tiled=True)  61.4 us
    all_to_all x1, waiting for transfers between devices, local(): lax.all_to_all(outgoing.reshape(EXPERTS, CAP, model_width), 'tok', split_...  60.2 us
    all_gather x1, waiting for transfers between devices, local(): lax.all_gather(columns, 'grp', axis=0, tiled=True)  55.2 us
    all_gather x1, blocking collectives, local(): columns = lax.all_gather(w_qkv, 'tok', axis=1, tiled=True)  35 us
    all_gather x1, blocking collectives, local(): lax.all_gather(prefix_cache[0], 'tok', axis=0, tiled=True)  31 us
    all_gather x1, blocking collectives, local(): out_columns = lax.all_gather(w_out, 'tok', axis=1, tiled=True)  30.6 us
    convert_element_type x1, local copies, waits for them, and re-layouts, local(): expert_result = jnp.einsum('erf,efd->erd', sliced, lax.all_gather(expert_...  18.2 us
  transfers between devices with their start and end apart: 7, of which 5 were waited for; matrix products, arithmetic and copies ran while one was open for 10% of the time, Pallas kernels for 0%

commit v1 on v0

--- a/solution.py
+++ b/solution.py
@@ -14,6 +14,12 @@
 score_scale = 0.015625
 rope_base = 10000.0
 big_negative = -1e30
+
+
+def stacked_exchange(shard, name, split, join):
+    pieces = jnp.split(shard, lax.axis_size(name), axis=split)
+    received = lax.all_to_all(jnp.stack(pieces), name, 0, 0)
+    return jnp.concatenate(received, axis=join)
 
 
 def rms_scale(values, gain):
@@ -177,9 +183,7 @@
         lax.all_gather(expert_down, "grp", axis=1, tiled=True),
         preferred_element_type=jnp.float32,
     ).astype(jnp.bfloat16)
-    returned = lax.all_to_all(
-        expert_result, "tok", split_axis=1, concat_axis=0, tiled=True
-    ).reshape(EXPERTS * CAP, -1)
+    returned = stacked_exchange(expert_result, "tok", 1, 0).reshape(EXPERTS * CAP, -1)
     weighted = returned[slot_index].astype(jnp.float32) * gates[0].reshape(-1)[:, None]
     moe_out = jnp.sum(weighted.reshape(tok_count, TOP, -1), axis=1)
     hidden_out = (after_attention + moe_out).astype(jnp.bfloat16)

time: 594 us -> 566 us (0.953)
  other arithmetic: 38.8 us -> 23.3 us
  local copies, waits for them, and re-layouts: 74.3 us -> 62.2 us
    convert_element_type x1 -> x0, local copies, waits for them, and re-layouts: 18.2 us -> none  [local(): expert_result = jnp.einsum('erf,efd->erd', sliced, lax.all_gather(expert_...]
    unnamed x1 -> x0, other arithmetic: 15.6 us -> none
    unnamed x26 -> x53, local copies, waits for them, and re-layouts: 17.1 us -> 22.5 us
  transfers between devices with their start and end apart: 7 -> 7, of which waited for: 5 -> 5; matrix products, arithmetic and copies ran while one was open for 10% -> 11% of each run, Pallas kernels for 0% -> 0%
where the time goes in v1:
time: 566 us
  waiting for transfers between devices  317 us (56%)
  blocking collectives  96.7 us (17%)
  local copies, waits for them, and re-layouts  62.2 us (11%)
  matrix products  32.4 us (6%)
  other arithmetic  23.3 us (4%)
  starting transfers between devices  19.9 us (4%)
  between operations  14.2 us (3%)
    all_to_all x1, waiting for transfers between devices, stacked_exchange(): received = lax.all_to_all(jnp.stack(pieces), name, 0, 0)  123 us
    all_gather x1, waiting for transfers between devices, local(): lax.all_gather(expert_gate_up, 'grp', axis=1, tiled=True)  61.4 us
    all_to_all x1, waiting for transfers between devices, local(): lax.all_to_all(outgoing.reshape(EXPERTS, CAP, model_width), 'tok', split_...  60.2 us
    all_gather x1, waiting for transfers between devices, local(): lax.all_gather(columns, 'grp', axis=0, tiled=True)  55.2 us
    all_gather x1, blocking collectives, local(): columns = lax.all_gather(w_qkv, 'tok', axis=1, tiled=True)  35 us
    all_gather x1, blocking collectives, local(): lax.all_gather(prefix_cache[0], 'tok', axis=0, tiled=True)  31 us
    all_gather x1, blocking collectives, local(): out_columns = lax.all_gather(w_out, 'tok', axis=1, tiled=True)  30.6 us
    unnamed x53, local copies, waits for them, and re-layouts  22.5 us
  transfers between devices with their start and end apart: 7, of which 5 were waited for; matrix products, arithmetic and copies ran while one was open for 11% of the time, Pallas kernels for 0%

profile of v1, /device:TPU:32, one launch (start us, length us, event | category | flops | bytes accessed | tf_op | source)
XLA Modules:
  0.0 565.7 jit_solution(14187997027213166854)
XLA Ops:
  7.2 35.0 %all_gather.24 = bf16[64,1024]{0,1:T(8,128)(2,1)S(1)} all-gather(bf16[64,32]{0,1:T(8,128)(2,1)} %param.17), channel_id=1, replica_groups=mesh['grp'=16,'tok'=32] {'tok'}, dimensions={1}, use_global_device_ids=true | all-gather | bytes 135168 | tf_op jit(solution)/shard_map/all_gather | solution.py:107
  43.1 0.8 reduce-window.10
  44.8 1.1 fusion.26
  46.1 55.2 %all-gather.7.cloned.1.call-done = bf16[1024,1024]{1,0:T(8,128)(2,1)} async-done(((bf16[64,1024]{1,0:T(8,128)(2,1)}), bf16[1024,1024]{1,0:T(8,128)(2,1)}) %all-gather.7.cloned.1.call-update) | async-done | bytes 2097168 | tf_op jit(solution)/shard_map/all_gather | solution.py:111
  101.3 2.2 fusion.30
  105.4 30.6 %all_gather.28 = bf16[32,1024]{0,1:T(8,128)(2,1)S(1)} all-gather(bf16[32,32]{0,1:T(8,128)(2,1)S(1)} %copy.96), channel_id=1, replica_groups=mesh['grp'=16,'tok'=32] {'tok'}, dimensions={1}, use_global_device_ids=true | all-gather | bytes 67584 | tf_op jit(solution)/shard_map/all_gather | solution.py:146
  137.7 2.4 broadcast_in_dim.41
  140.2 2.6 broadcast_in_dim.42
  142.7 31.0 %all-gather = bf16[1,512,512]{2,1,0:T(8,128)(2,1)S(1)} all-gather(bf16[1,16,512]{2,1,0:T(8,128)(2,1)S(1)} %copy-done.5), channel_id=2, replica_groups=mesh['grp'=16,'tok'=32] {'tok'}, dimensions={1}, use_global_device_ids=true | all-gather | bytes 540672 | tf_op jit(solution)/shard_map/all_gather | solution.py:135
  174.0 0.9 copy.88
  175.0 9.2 %reduce-window.11 = s32[32,8,128]{2,1,0:T(8,128)S(1)} reduce-window(s32[32,8,128]{2,1,0:T(8,128)S(1)} %fusion.37, s32[]{:T(128)} %constant.34.clone.1), window={size=1x1x128 pad=0_0x0_0x127_0}, to_apply=%region_9.10 | reduce-window | flops 4161536 | bytes 262148 | tf_op jit(solution)/shard_map/reduce-window.1
  186.0 1.8 multiply_reduce_fusion
  187.8 3.8 fusion.77
  191.6 2.9 copy.93
  194.6 2.9 copy.91
  197.5 3.5 fusion
  201.0 4.4 fusion.1
  205.4 1.9 copy-done
  207.9 11.2 %fusion.3 = f32[4,256,64]{1,2,0:T(8,128)} fusion(bf16[4,4096,64]{1,2,0:T(8,128)(2,1)} %bitcast.225, f32[4,256,4096]{2,1,0:T(8,128)} %copy-done, f32[4,256]{1,0:T(4,128)S(1)} %get-tuple-element.15, pred[256,4096]{1,0:T(8,128)(4,1)S(1)} %broadcast_in_dim.42), kind=kOutput, calls=%fused_computation.8 | convolution fusion | flops 553648128 | bytes 20189184 | tf_op jit(solution)/shard_map/kqn,knd->kqd/dot_general | solution.py:76
  219.1 1.6 fusion.21
  221.0 16.5 %all-gather.11.cloned.1.call-done = bf16[512,1024]{1,0:T(8,128)(2,1)} async-done(((bf16[32,1024]{1,0:T(8,128)(2,1)}), bf16[512,1024]{1,0:T(8,128)(2,1)}) %all-gather.11.cloned.1.call-update) | async-done | bytes 1048592 | tf_op jit(solution)/shard_map/all_gather | solution.py:150
  237.6 1.6 multiply_reduce_fusion.1
  239.3 14.7 %scatter_custom_fusion = bf16[1280,1024]{1,0:T(8,128)(2,1)} fusion(s32[1024]{0:T(1024)S(1)} %bitcast.238, bf16[128,1024]{1,0:T(8,128)(2,1)S(1)} %multiply_convert_fusion, s32[1024]{0:T(1024)S(1)} %broadcast_clamp_fusion.1, bf16[]{:T(256)} %constant.67.clone.1), kind=kCustom, calls=%fused_computation.18 | custom fusion | bytes 2621442 | tf_op jit(solution)/shard_map/scatter | solution.py:166
  254.1 12.8 %all-to-all-start = ((bf16[32,40,1024]{2,1,0:T(8,128)(2,1)}), bf16[32,40,1024]{2,1,0:T(8,128)(2,1)S(1)}, u32[]{:S(2)}, u32[]{:S(2)}) async-start(bf16[32,40,1024]{2,1,0:T(8,128)(2,1)} %bitcast.31), calls=%async_computation | async-start | bytes 5242880 | tf_op jit(solution)/shard_map/all_to_all | solution.py:168
  268.0 61.4 %all-gather.13.cloned.1.call-done = bf16[1,1024,1024]{2,1,0:T(8,128)(2,1)} async-done(((bf16[1,64,1024]{2,1,0:T(8,128)(2,1)}), bf16[1,1024,1024]{2,1,0:T(8,128)(2,1)}) %all-gather.13.cloned.1.call-update) | async-done | bytes 2097168 | tf_op jit(solution)/shard_map/all_gather | solution.py:175
  329.4 60.2 %all-to-all-done = bf16[32,40,1024]{2,1,0:T(8,128)(2,1)S(1)} async-done(((bf16[32,40,1024]{2,1,0:T(8,128)(2,1)}), bf16[32,40,1024]{2,1,0:T(8,128)(2,1)S(1)}, u32[]{:S(2)}, u32[]{:S(2)}) %all-to-all-start) | async-done | bytes 2621472 | tf_op jit(solution)/shard_map/all_to_all | solution.py:168
  389.6 6.2 %convolution_bitcast_fusion = f32[1,1280,1024]{2,1,0:T(8,128)} fusion(bf16[1280,1024]{1,0:T(8,128)(2,1)S(1)} %bitcast.224, bf16[1,1024,1024]{2,1,0:T(8,128)(2,1)} %all-gather.13.cloned.1.call-done), kind=kOutput, calls=%fused_computation.10 | convolution fusion | flops 2684354560 | bytes 9961472 | tf_op jit(solution)/shard_map/erd,edf->erf/dot_general | solution.py:172
  395.8 4.4 fusion.7
  420.5 6.9 %all-to-all-start.1 = ((bf16[32,1,40,1024]{3,2,1,0:T(8,128)(2,1)}), bf16[32,1,40,1024]{3,2,1,0:T(8,128)(2,1)S(1)}, u32[]{:S(2)}, u32[]{:S(2)}) async-start(bf16[32,1,40,1024]{3,2,1,0:T(8,128)(2,1)} %fusion.38), calls=%async_computation.1 | async-start | bytes 5242880 | tf_op jit(solution)/shard_map/all_to_all | solution.py:21
  427.5 122.6 %all-to-all-done.1 = bf16[32,1,40,1024]{3,2,1,0:T(8,128)(2,1)S(1)} async-done(((bf16[32,1,40,1024]{3,2,1,0:T(8,128)(2,1)}), bf16[32,1,40,1024]{3,2,1,0:T(8,128)(2,1)S(1)}, u32[]{:S(2)}, u32[]{:S(2)}) %all-to-all-start.1) | async-done | bytes 2621472 | tf_op jit(solution)/shard_map/all_to_all | solution.py:21
  550.1 5.4 gather_fusion
  555.5 2.9 fusion.6
  (120 shorter events, 30.8 us)
Async XLA Ops:
  7.2 94.1 %all-gather.7.cloned.1.call-start = ((), (), s32[]{:S(2)}) async-start(), calls=%async_computation.2 | async-start | bytes 2228224 | tf_op jit(solution)/shard_map/all_gather | solution.py:111
  42.3 63.1 %copy-start.7 = (bf16[32,32]{1,0:T(8,128)(2,1)S(1)}, bf16[32,32]{1,0:T(8,128)(2,1)}, u32[]{:S(2)}) copy-start(bf16[32,32]{1,0:T(8,128)(2,1)} %param.18) | copy-start | bytes 6148
  43.1 144.7 %all-gather.9.cloned.1.call-start = ((), (), s32[]{:S(2)}) async-start(), calls=%async_computation.3 | async-start | bytes 4325376 | tf_op jit(solution)/shard_map/all_gather | solution.py:137
  46.1 90.9 %copy-start.6 = (s32[1,128,8]{1,2,0:T(8,128)S(1)}, s32[1,128,8]{1,2,0:T(8,128)}, u32[]{:S(2)}) copy-start(s32[1,128,8]{1,2,0:T(8,128)} %param.14) | copy-start | bytes 12292
  103.5 0.8 copy-start.3
  105.3 132.3 %all-gather.11.cloned.1.call-start = ((), (), s32[]{:S(2)}) async-start(), calls=%async_computation.4 | async-start | bytes 1114112 | tf_op jit(solution)/shard_map/all_gather | solution.py:150
  137.7 5.0 copy-start.5
  142.7 42.0 %slice-start = ((f32[128,1024]{1,0:T(8,128)}), f32[128,512]{1,0:T(8,128)S(1)}, s32[]{:S(2)}) async-start(f32[128,1024]{1,0:T(8,128)} %copy-done.3), calls=%async_computation.7 | async-start | bytes 524288 | tf_op jit(solution)/shard_map/slice | solution.py:114
  201.0 6.3 %copy-start = (f32[4,256,4096]{2,1,0:T(8,128)}, f32[4,256,4096]{2,1,0:T(8,128)S(1)}, u32[]{:S(2)}) copy-start(f32[4,256,4096]{2,1,0:T(8,128)S(1)} %get-tuple-element.22) | copy-start | bytes 50331652
  201.0 6.3 %copy-start.1 = (f32[4,256,512]{2,1,0:T(8,128)S(1)}, f32[4,256,512]{2,1,0:T(8,128)}, u32[]{:S(2)}) copy-start(f32[4,256,512]{2,1,0:T(8,128)} %get-tuple-element.20) | copy-start | bytes 6291460
  207.9 11.2 %copy-start.4 = (bf16[512,256]{0,1:T(8,128)(2,1)S(1)}, bf16[512,256]{0,1:T(8,128)(2,1)}, u32[]{:S(2)}) copy-start(bf16[512,256]{0,1:T(8,128)(2,1)} %copy.88) | copy-start | bytes 786436
  219.1 18.4 %copy-start.2 = (bf16[1,128,1024]{2,1,0:T(8,128)(2,1)S(1)}, bf16[1,128,1024]{2,1,0:T(8,128)(2,1)}, u32[]{:S(2)}) copy-start(bf16[1,128,1024]{2,1,0:T(8,128)(2,1)} %param.11) | copy-start | bytes 786436
  219.1 20.1 %copy-start.8 = (f32[1024]{0:T(1024)S(1)}, f32[1024]{0:T(1024)}, u32[]{:S(2)}) copy-start(f32[1024]{0:T(1024)} %param.19) | copy-start | bytes 12292
  254.1 135.6 %all-to-all-start = ((bf16[32,40,1024]{2,1,0:T(8,128)(2,1)}), bf16[32,40,1024]{2,1,0:T(8,128)(2,1)S(1)}, u32[]{:S(2)}, u32[]{:S(2)}) async-start(bf16[32,40,1024]{2,1,0:T(8,128)(2,1)} %bitcast.31), calls=%async_computation | async-start | bytes 5242880 | tf_op jit(solution)/shard_map/all_to_all | solution.py:168
  266.9 62.5 %all-gather.13.cloned.1.call-start = ((), (), s32[]{:S(2)}) async-start(), calls=%async_computation.5 | async-start | bytes 2228224 | tf_op jit(solution)/shard_map/all_gather | solution.py:175
  267.5 128.3 %all-gather.15.cloned.1.call-start = ((), (), s32[]{:S(2)}) async-start(), calls=%async_computation.6 | async-start | bytes 1114112 | tf_op jit(solution)/shard_map/all_gather | solution.py:183
  420.5 6.9 %copy-start.9 = (f32[1,128,8]{1,2,0:T(8,128)S(1)}, f32[1,128,8]{1,2,0:T(8,128)}, u32[]{:S(2)}) copy-start(f32[1,128,8]{1,2,0:T(8,128)} %param.15) | copy-start | bytes 12292
  420.5 129.7 %all-to-all-start.1 = ((bf16[32,1,40,1024]{3,2,1,0:T(8,128)(2,1)}), bf16[32,1,40,1024]{3,2,1,0:T(8,128)(2,1)S(1)}, u32[]{:S(2)}, u32[]{:S(2)}) async-start(bf16[32,1,40,1024]{3,2,1,0:T(8,128)(2,1)} %fusion.38), calls=%async_computation.1 | async-start | bytes 5242880 | tf_op jit(solution)/shard_map/all_to_all | solution.py:21
Sparse Core Ops, SparseCore 0:
  43.2 58.0 all-gather.6
  105.4 73.6 all-gather.8
  182.1 55.3 all-gather.10
  270.4 58.9 all-gather.12
  332.3 57.4 all-gather.14
